TPU v7x, 32 devices: a whole 2x2x4 slice. The times are simulated.
32 devices in a mesh: section: 2 (over x), expert: 16 (over z, y, core).
Axes of the slice: x: 2, y: 2, z: 4, core: 2. Of those that a mesh axis runs over, the one named last changes fastest.
Arguments:
- tokens: bfloat16 [2, 256, 2048], P('section', 'expert'), may hold values from -6 to 6
- out_grad: bfloat16 [2, 256, 2048], P('section', 'expert'), may hold values from -1 to 1
- expert_ids: int32 [2, 256, 2], P('section'), may hold values from 0 to 3, all different within a row; in each aligned block of 16 rows (0 to 15, 16 to 31, ..., all dimensions but the last counted through in order) at most 14 rows name the same one
- gate_weights: bfloat16 [2, 256, 2], P('section'), may hold values from 0.049804688 to 1
- gate_up_rows: bfloat16 [2, 16, 384, 2048], P('section', 'expert'), may hold values from -0.125 to 0.125
- down_rows: bfloat16 [2, 16, 192, 2048], P('section', 'expert'), may hold values from -0.21875 to 0.21875
Outputs:
- gate_grad: float32 [2, 256, 2], P('section', 'expert')
- handed: bfloat16 [2, 256, 2048], P('section', 'expert')
Inputs may be any that keep to these rules, and one draw needn't show every extreme that they name: `expert_ids`: within the rows of one device (16 consecutive rows of a section), every expert id appears in at most 14 rows, and some id reaches 14; the 2 ids of a row are distinct.
All inputs are finite; a program needn't handle non-finite values.
Results may differ from a plain program's by a relative error of at most 0.0049.
Values may be sent and summed in bfloat16 or wider, within the bound.
No kernel may reach another device: no remote copies, remote signals or barrier semaphores. Data moves between devices by JAX's collectives and lax.ppermute only.
A program may use at most 64 MiB of HBM per device.

v0:
```python
import jax
import jax.numpy as jnp
from jax import lax
from jax.sharding import PartitionSpec as P


def from_behind(shard, axis, by):
    length = lax.axis_size(axis)
    pairs = [(i, i + by) for i in range(length) if 0 <= i + by < length]
    return lax.ppermute(shard, axis, pairs)


def slot_table(matches, capacity):
    ranked = jnp.cumsum(matches, axis=-1) - 1.0
    levels = jnp.arange(capacity, dtype=jnp.float32)
    return matches[..., None, :] * (ranked[..., None, :] == levels[:, None]).astype(jnp.float32)


def expert_grads(rows_in, rows_grad, slot_gate, gate_up, down_mat):
    width = down_mat.shape[0]
    contract = (((1,), (1,)), ((), ()))
    both = lax.dot_general(rows_in, gate_up, contract, preferred_element_type=jnp.float32)
    first = both[:, :width]
    second = both[:, width:]
    back = lax.dot_general(rows_grad, down_mat, contract, preferred_element_type=jnp.float32)
    sigma = jax.nn.sigmoid(first)
    active = first * sigma
    slot_grad = jnp.sum(back * active * second, axis=1)
    scaled = slot_gate[:, None] * back
    d_first = scaled * second * sigma * (1.0 + first * (1.0 - sigma))
    d_second = scaled * active
    d_both = jnp.concatenate([d_first, d_second], axis=1).astype(jnp.bfloat16)
    contrib = jnp.dot(d_both, gate_up, preferred_element_type=jnp.float32)
    return (contrib, slot_grad)


def body(tokens, out_grad, expert_ids, gate_weights, gate_up_rows, down_rows):
    group_size = lax.axis_size("expert")
    expert_count = max(2, group_size // 4)
    part_count = group_size // expert_count
    position = lax.axis_index("expert")
    my_expert = position // part_count
    block_rows = tokens.shape[1]
    model_width = tokens.shape[2]
    route_count = expert_ids.shape[2]
    pairs = block_rows * route_count
    capacity = min(block_rows, max(2, 7 * block_rows * route_count // (4 * expert_count)))
    gate_up = gate_up_rows[0, 0]
    down_mat = down_rows[0, 0]
    all_ids = expert_ids[0]
    all_gates = gate_weights[0].astype(jnp.float32)
    highest = lax.Precision.HIGHEST
    all_in, all_grad = (
        lax.all_gather(tokens[0], "expert", axis=0, tiled=True),
        lax.all_gather(out_grad[0], "expert", axis=0, tiled=True),
    )
    matches = (all_ids.reshape(group_size, pairs) == my_expert).astype(jnp.float32)
    slot_pick = slot_table(matches, capacity)
    chooser = slot_pick.reshape(group_size, capacity, block_rows, route_count).sum(axis=-1)
    slot_gate = jnp.sum(slot_pick * all_gates.reshape(group_size, 1, pairs), axis=-1)
    chooser_half = chooser.astype(jnp.bfloat16)
    rows_in = jnp.einsum(
        "jrt,jtd->jrd",
        chooser_half,
        all_in.reshape(group_size, block_rows, model_width),
        preferred_element_type=jnp.float32,
    ).astype(jnp.bfloat16)
    rows_grad = jnp.einsum(
        "jrt,jtd->jrd",
        chooser_half,
        all_grad.reshape(group_size, block_rows, model_width),
        preferred_element_type=jnp.float32,
    ).astype(jnp.bfloat16)
    contrib, slot_grad = expert_grads(
        rows_in.reshape(-1, model_width),
        rows_grad.reshape(-1, model_width),
        slot_gate.reshape(-1),
        gate_up,
        down_mat,
    )
    partial_value = jnp.einsum(
        "jrt,jrd->jtd",
        chooser,
        contrib.reshape(group_size, capacity, model_width),
        precision=highest,
    ).reshape(group_size * block_rows, model_width)
    gate_part = jnp.einsum(
        "jrp,jr->jp", slot_pick, slot_grad.reshape(group_size, capacity), precision=highest
    ).reshape(group_size * block_rows, route_count)
    grad_rows, gate_grad = (
        lax.psum_scatter(partial_value, "expert", scatter_dimension=0, tiled=True),
        lax.psum_scatter(gate_part, "expert", scatter_dimension=0, tiled=True),
    )
    handed = from_behind(grad_rows.astype(jnp.bfloat16), "section", -1)
    return (gate_grad[None], handed[None])


def solution(mesh):
    return jax.shard_map(
        body,
        mesh=mesh,
        in_specs=(
            P("section", "expert", None),
            P("section", "expert", None),
            P("section", None, None),
            P("section", None, None),
            P("section", "expert", None, None),
            P("section", "expert", None, None),
        ),
        out_specs=(P("section", "expert", None), P("section", "expert", None)),
        check_vma=False,
    )
```

profile of v0, /device:TPU:0, one launch (start us, length us, event | category | flops | bytes accessed | tf_op | source)
XLA Modules:
  0.0 227.0 jit_solution(1445343976378787823)
XLA Ops:
  7.2 0.7 all-gather.7.cloned.1.call-update
  8.0 0.7 all-gather.5.cloned.1.call-update
  8.7 0.7 compare_convert_fusion
  10.3 0.6 copy-done.1
  10.9 0.8 copy.48
  11.9 0.7 multiply_reduce_fusion.1
  12.7 38.2 %all-gather.7.cloned.1.call-done = bf16[1,256,2048]{2,1,0:T(8,128)(2,1)} async-done(((bf16[1,16,2048]{2,1,0:T(8,128)(2,1)}), bf16[1,256,2048]{2,1,0:T(8,128)(2,1)}) %all-gather.7.cloned.1.call-update) | async-done | bytes 1048592 | tf_op jit(solution)/shard_map/all_gather | solution.py:54
  50.9 1.6 convolution_convert_fusion
  52.8 37.1 %all-gather.5.cloned.1.call-done = bf16[1,256,2048]{2,1,0:T(8,128)(2,1)} async-done(((bf16[1,16,2048]{2,1,0:T(8,128)(2,1)}), bf16[1,256,2048]{2,1,0:T(8,128)(2,1)}) %all-gather.5.cloned.1.call-update) | async-done | bytes 1048592 | tf_op jit(solution)/shard_map/all_gather | solution.py:55
  89.9 1.7 convolution_convert_fusion.1
  91.6 1.2 reshape.84
  92.8 0.6 fusion.2
  93.4 0.6 copy-done.3
  94.2 0.5 multiply_convert_fusion.1
  95.0 0.7 fusion
  95.8 3.3 %fusion.12 = f32[16,16,2048]{2,1,0:T(8,128)} fusion(f32[16,14,2048]{2,1,0:T(8,128)S(1)} %fusion, f32[16,14,16]{2,0,1:T(8,128)S(1)} %copy-done.2), kind=kOutput, calls=%fused_computation.20 | convolution fusion | flops 88080384 | bytes 3946496 | tf_op jit(solution)/shard_map/jrt,jrd->jtd/dot_general | solution.py:81
  99.3 60.5 %reduce-scatter.5.cloned.1.call-done = f32[16,2048]{1,0:T(8,128)} async-done(((f32[256,2048]{1,0:T(8,128)}), f32[16,2048]{1,0:T(8,128)}) %reduce-scatter.5.cloned.1.call-update) | async-done | bytes 131088 | tf_op jit(solution)/shard_map/reduce_scatter | solution.py:91
  159.8 0.9 convert_element_type.62
  160.7 1.3 collective-permute-start
  162.0 0.3 fusion.10
  162.3 0.7 reshape.88
  163.1 55.4 %reduce-scatter.3.cloned.1.call-done = f32[16,2]{1,0:T(8,128)} async-done(((f32[256,2]{1,0:T(8,128)}), f32[16,2]{1,0:T(8,128)}) %reduce-scatter.3.cloned.1.call-update) | async-done | bytes 144 | tf_op jit(solution)/shard_map/reduce_scatter | solution.py:92
  218.5 1.3 copy.47
  219.8 0.6 copy.66
  (38 shorter events, 2.3 us)
Async XLA Ops:
  7.2 85.6 %copy-start = (bf16[1,1,384,2048]{3,2,1,0:T(8,128)(2,1)S(1)}, bf16[1,1,384,2048]{3,2,1,0:T(8,128)(2,1)}, u32[]{:S(2)}) copy-start(bf16[1,1,384,2048]{3,2,1,0:T(8,128)(2,1)} %param.10) | copy-start | bytes 4718596
  7.2 43.7 %all-gather.7.cloned.1.call-start = ((), (), s32[]{:S(2)}) async-start(), calls=%async_computation.5 | async-start | bytes 1114112 | tf_op jit(solution)/shard_map/all_gather | solution.py:54
  7.9 82.0 %all-gather.5.cloned.1.call-start = ((), (), s32[]{:S(2)}) async-start(), calls=%async_computation.4 | async-start | bytes 1114112 | tf_op jit(solution)/shard_map/all_gather | solution.py:55
  8.7 151.2 %reduce-scatter.5.cloned.1.call-start = ((), (), s32[]{:S(2)}) async-start(), calls=%async_computation.3 | async-start | bytes 2228224 | tf_op jit(solution)/shard_map/reduce_scatter | solution.py:91
  10.3 0.7 copy-start.1
  10.9 39.9 %copy-start.4 = (bf16[16,14,16]{2,0,1:T(8,128)(2,1)}, bf16[16,14,16]{2,0,1:T(8,128)(2,1)S(1)}, u32[]{:S(2)}) copy-start(bf16[16,14,16]{2,0,1:T(8,128)(2,1)S(1)} %convert_element_type.57) | copy-start | bytes 21508
  92.8 1.2 copy-start.3
  92.8 1.4 copy-start.6
  94.9 0.9 copy-start.2
  99.1 62.9 %copy-start.5 = (f32[16,14,32]{2,0,1:T(8,128)S(1)}, f32[16,14,32]{2,0,1:T(8,128)}, u32[]{:S(2)}) copy-start(f32[16,14,32]{2,0,1:T(8,128)} %get-tuple-element.6) | copy-start | bytes 86020
  99.2 119.3 %reduce-scatter.3.cloned.1.call-start = ((), (), s32[]{:S(2)}) async-start(), calls=%async_computation.2 | async-start | bytes 139264 | tf_op jit(solution)/shard_map/reduce_scatter | solution.py:92
  160.7 59.1 %collective-permute-start = (bf16[16,2048]{1,0:T(8,128)(2,1)S(1)}, bf16[16,2048]{1,0:T(8,128)(2,1)S(1)}, u32[]{:S(2)}, u32[]{:S(2)}) collective-permute-start(bf16[16,2048]{1,0:T(8,128)(2,1)S(1)} %convert_element_type.62), channel_id=1, source_target_pairs={{16,0},{17,1},{18,2},{19,3},{20,4},{21,5},{22,6},{23,7},{24,8},{25... | collective-permute-start | bytes 196616 | tf_op jit(solution)/shard_map/ppermute | solution.py:10
Sparse Core Ops, SparseCore 0:
  10.2 40.6 all-gather.6
  53.0 36.8 all-gather.4
  99.3 60.4 reduce-scatter.4
  163.5 54.9 reduce-scatter.2
where the time goes:
time: 227 us
  waiting for transfers between devices  193 us (85%)
  between operations  13.9 us (6%)
  matrix products  8.71 us (4%)
  local copies, waits for them, and re-layouts  7.79 us (3%)
  other arithmetic  2.49 us (1%)
    reduce_scatter x1, waiting for transfers between devices, body(): lax.psum_scatter(partial_value, 'expert', scatter_dimension=0, tiled=True)  60.5 us
    reduce_scatter x1, waiting for transfers between devices, body(): lax.psum_scatter(gate_part, 'expert', scatter_dimension=0, tiled=True)  55.4 us
    all_gather x1, waiting for transfers between devices, body(): lax.all_gather(tokens[0], 'expert', axis=0, tiled=True)  38.2 us
    all_gather x1, waiting for transfers between devices, body(): lax.all_gather(out_grad[0], 'expert', axis=0, tiled=True)  37.1 us
  transfers between devices with their start and end apart: 5, of which 4 were waited for; matrix products, arithmetic and copies ran while one was open for 3% of the time, Pallas kernels for 0%

commit v1 on v0

--- a/solution.py
+++ b/solution.py
@@ -2,6 +2,18 @@
 import jax.numpy as jnp
 from jax import lax
 from jax.sharding import PartitionSpec as P
+
+
+def doubled_up(x, axis, dim):
+    ways, here, step = (lax.axis_size(axis), lax.axis_index(axis), x.shape[dim])
+    line, have = (x, 1)
+    while have < ways:
+        line = jnp.concatenate(
+            [line, lax.ppermute(line, axis, [(d, (d - have) % ways) for d in range(ways)])],
+            axis=dim,
+        )
+        have = 2 * have
+    return jnp.roll(line, here * step, axis=dim)
 
 
 def from_behind(shard, axis, by):
@@ -51,7 +63,7 @@
     all_gates = gate_weights[0].astype(jnp.float32)
     highest = lax.Precision.HIGHEST
     all_in, all_grad = (
-        lax.all_gather(tokens[0], "expert", axis=0, tiled=True),
+        doubled_up(tokens[0], "expert", 0),
         lax.all_gather(out_grad[0], "expert", axis=0, tiled=True),
     )
     matches = (all_ids.reshape(group_size, pairs) == my_expert).astype(jnp.float32)

time: 227 us -> 202 us (0.89)
  waiting for transfers between devices: 193 us -> 158 us
  starting transfers between devices: 1.44 us -> 9.91 us
    ppermute x0 -> x4, waiting for transfers between devices: none -> 41.4 us  [doubled_up(): lax.ppermute(line, axis, [(d, (d - have) % ways) for d in range(ways)])]
    all_gather x1 -> x0, waiting for transfers between devices: 38.2 us -> none  [body(): lax.all_gather(tokens[0], 'expert', axis=0, tiled=True)]
    all_gather x1, waiting for transfers between devices: 37.1 us -> 0.01 us  [body(): lax.all_gather(out_grad[0], 'expert', axis=0, tiled=True)]
    ppermute x0 -> x4, starting transfers between devices: none -> 8.51 us  [doubled_up(): lax.ppermute(line, axis, [(d, (d - have) % ways) for d in range(ways)])]
  transfers between devices with their start and end apart: 5 -> 8, of which waited for: 4 -> 5; matrix products, arithmetic and copies ran while one was open for 3% -> 5% of each run, Pallas kernels for 0% -> 0%
where the time goes in v1:
time: 202 us
  waiting for transfers between devices  158 us (78%)
  between operations  14.1 us (7%)
  starting transfers between devices  9.91 us (5%)
  matrix products  9.56 us (5%)
  local copies, waits for them, and re-layouts  5.69 us (3%)
  other arithmetic  4.22 us (2%)
    reduce_scatter x1, waiting for transfers between devices, body(): lax.psum_scatter(partial_value, 'expert', scatter_dimension=0, tiled=True)  61.5 us
    reduce_scatter x1, waiting for transfers between devices, body(): lax.psum_scatter(gate_part, 'expert', scatter_dimension=0, tiled=True)  55.4 us
    ppermute x4, waiting for transfers between devices, doubled_up(): lax.ppermute(line, axis, [(d, (d - have) % ways) for d in range(ways)])  41.4 us
    ppermute x4, starting transfers between devices, doubled_up(): lax.ppermute(line, axis, [(d, (d - have) % ways) for d in range(ways)])  8.51 us
  transfers between devices with their start and end apart: 8, of which 5 were waited for; matrix products, arithmetic and copies ran while one was open for 5% of the time, Pallas kernels for 0%

profile of v1, /device:TPU:0, one launch (start us, length us, event | category | flops | bytes accessed | tf_op | source)
XLA Modules:
  0.0 201.8 jit_solution(3131588610471445215)
XLA Ops:
  7.2 5.5 %collective-permute-start = (bf16[16,2048]{1,0:T(8,128)(2,1)}, bf16[16,2048]{1,0:T(8,128)(2,1)S(1)}, u32[]{:S(2)}, u32[]{:S(2)}) collective-permute-start(bf16[16,2048]{1,0:T(8,128)(2,1)} %bitcast.36), channel_id=1, source_target_pairs={{0,15},{1,0},{2,1},{3,2},{4,3},{5,4},{6,5},{7,6},{8,7},{9,8},{10,9... | collective-permute-start | bytes 196616 | tf_op jit(solution)/shard_map/ppermute | solution.py:12
  12.8 0.7 compare_convert_fusion
  14.4 0.8 copy.48
  15.4 0.9 pad_maximum_fusion.2
  16.2 1.2 collective-permute-start.1
  17.4 0.6 multiply_reduce_fusion.1
  18.3 3.0 %collective-permute-done.1 = bf16[32,2048]{1,0:T(8,128)(2,1)S(1)} collective-permute-done((bf16[32,2048]{1,0:T(8,128)(2,1)S(1)}, bf16[32,2048]{1,0:T(8,128)(2,1)S(1)}, u32[]{:S(2)}, u32[]{:S(2)}) %collective-permute-start.1) | collective-permute-done | bytes 131104 | tf_op jit(solution)/shard_map/ppermute | solution.py:12
  21.2 0.9 pad_maximum_fusion.1
  22.1 0.5 collective-permute-start.2
  22.6 9.1 %collective-permute-done.2 = bf16[64,2048]{1,0:T(8,128)(2,1)S(1)} collective-permute-done((bf16[64,2048]{1,0:T(8,128)(2,1)S(1)}, bf16[64,2048]{1,0:T(8,128)(2,1)S(1)}, u32[]{:S(2)}, u32[]{:S(2)}) %collective-permute-start.2) | collective-permute-done | bytes 262176 | tf_op jit(solution)/shard_map/ppermute | solution.py:12
  31.7 1.3 collective-permute-start.3
  33.1 29.4 %collective-permute-done.3 = bf16[128,2048]{1,0:T(8,128)(2,1)S(1)} collective-permute-done((bf16[128,2048]{1,0:T(8,128)(2,1)S(1)}, bf16[128,2048]{1,0:T(8,128)(2,1)S(1)}, u32[]{:S(2)}, u32[]{:S(2)}) %collective-permute-start.3) | collective-permute-done | bytes 524320 | tf_op jit(solution)/shard_map/ppermute | solution.py:12
  63.4 1.4 fusion.2
  64.8 1.7 convolution_convert_fusion.1
  66.7 1.8 multiply_convert_fusion.1
  68.8 0.7 fusion
  69.7 3.3 %fusion.12 = f32[16,16,2048]{2,1,0:T(8,128)} fusion(f32[16,14,2048]{2,1,0:T(8,128)S(1)} %fusion, f32[16,14,16]{2,0,1:T(8,128)S(1)} %copy-done.3), kind=kOutput, calls=%fused_computation.23 | convolution fusion | flops 88080384 | bytes 3946496 | tf_op jit(solution)/shard_map/jrt,jrd->jtd/dot_general | solution.py:93
  73.1 61.5 %reduce-scatter.5.cloned.1.call-done = f32[16,2048]{1,0:T(8,128)} async-done(((f32[256,2048]{1,0:T(8,128)}), f32[16,2048]{1,0:T(8,128)}) %reduce-scatter.5.cloned.1.call-update) | async-done | bytes 131088 | tf_op jit(solution)/shard_map/reduce_scatter | solution.py:103
  134.6 0.9 convert_element_type.62
  135.5 1.3 collective-permute-start.4
  137.1 0.7 reshape.88
  137.9 55.4 %reduce-scatter.3.cloned.1.call-done = f32[16,2]{1,0:T(8,128)} async-done(((f32[256,2]{1,0:T(8,128)}), f32[16,2]{1,0:T(8,128)}) %reduce-scatter.3.cloned.1.call-update) | async-done | bytes 144 | tf_op jit(solution)/shard_map/reduce_scatter | solution.py:104
  193.3 1.3 copy.47
  194.6 0.6 copy.75
  (55 shorter events, 3.3 us)
Async XLA Ops:
  7.2 56.3 %copy-start = (bf16[1,1,384,2048]{3,2,1,0:T(8,128)(2,1)S(1)}, bf16[1,1,384,2048]{3,2,1,0:T(8,128)(2,1)}, u32[]{:S(2)}) copy-start(bf16[1,1,384,2048]{3,2,1,0:T(8,128)(2,1)} %param.10) | copy-start | bytes 4718596
  7.2 15.4 %copy-start.1 = (bf16[1,16,2048]{2,1,0:T(8,128)(2,1)S(1)}, bf16[1,16,2048]{2,1,0:T(8,128)(2,1)}, u32[]{:S(2)}) copy-start(bf16[1,16,2048]{2,1,0:T(8,128)(2,1)} %param.6) | copy-start | bytes 196612
  7.2 57.6 %all-gather.3.cloned.1.call-start = ((), (), s32[]{:S(2)}) async-start(), calls=%async_computation.4 | async-start | bytes 1114112 | tf_op jit(solution)/shard_map/all_gather | solution.py:67
  7.2 8.1 %collective-permute-start = (bf16[16,2048]{1,0:T(8,128)(2,1)}, bf16[16,2048]{1,0:T(8,128)(2,1)S(1)}, u32[]{:S(2)}, u32[]{:S(2)}) collective-permute-start(bf16[16,2048]{1,0:T(8,128)(2,1)} %bitcast.36), channel_id=1, source_target_pairs={{0,15},{1,0},{2,1},{3,2},{4,3},{5,4},{6,5},{7,6},{8,7},{9,8},{10,9... | collective-permute-start | bytes 196616 | tf_op jit(solution)/shard_map/ppermute | solution.py:12
  12.8 121.9 %reduce-scatter.5.cloned.1.call-start = ((), (), s32[]{:S(2)}) async-start(), calls=%async_computation.3 | async-start | bytes 2228224 | tf_op jit(solution)/shard_map/reduce_scatter | solution.py:103
  14.4 1.0 copy-start.2
  14.4 48.3 %copy-start.4 = (bf16[16,14,16]{2,0,1:T(8,128)(2,1)}, bf16[16,14,16]{2,0,1:T(8,128)(2,1)S(1)}, u32[]{:S(2)}) copy-start(bf16[16,14,16]{2,0,1:T(8,128)(2,1)S(1)} %convert_element_type.57) | copy-start | bytes 21508
  16.2 5.0 %collective-permute-start.1 = (bf16[32,2048]{1,0:T(8,128)(2,1)S(1)}, bf16[32,2048]{1,0:T(8,128)(2,1)S(1)}, u32[]{:S(2)}, u32[]{:S(2)}) collective-permute-start(bf16[32,2048]{1,0:T(8,128)(2,1)S(1)} %pad_maximum_fusion.2), channel_id=1, source_target_pairs={{0,14},{1,15},{2,0},{3,1},{4,2},{5,3},{6,4},{7,5},{8,6},{9,7},{10,... | collective-permute-start | bytes 393224 | tf_op jit(solution)/shard_map/ppermute | solution.py:12
  22.1 9.6 %collective-permute-start.2 = (bf16[64,2048]{1,0:T(8,128)(2,1)S(1)}, bf16[64,2048]{1,0:T(8,128)(2,1)S(1)}, u32[]{:S(2)}, u32[]{:S(2)}) collective-permute-start(bf16[64,2048]{1,0:T(8,128)(2,1)S(1)} %pad_maximum_fusion.1), channel_id=1, source_target_pairs={{0,12},{1,13},{2,14},{3,15},{4,0},{5,1},{6,2},{7,3},{8,4},{9,5},{1... | collective-permute-start | bytes 786440 | tf_op jit(solution)/shard_map/ppermute | solution.py:12
  31.7 30.7 %collective-permute-start.3 = (bf16[128,2048]{1,0:T(8,128)(2,1)S(1)}, bf16[128,2048]{1,0:T(8,128)(2,1)S(1)}, u32[]{:S(2)}, u32[]{:S(2)}) collective-permute-start(bf16[128,2048]{1,0:T(8,128)(2,1)S(1)} %pad_maximum_fusion), channel_id=1, source_target_pairs={{0,8},{1,9},{2,10},{3,11},{4,12},{5,13},{6,14},{7,15},{8,0},{9,1},... | collective-permute-start | bytes 1572872 | tf_op jit(solution)/shard_map/ppermute | solution.py:12
  68.8 0.9 copy-start.3
  73.0 63.9 %copy-start.5 = (f32[16,14,32]{2,0,1:T(8,128)S(1)}, f32[16,14,32]{2,0,1:T(8,128)}, u32[]{:S(2)}) copy-start(f32[16,14,32]{2,0,1:T(8,128)} %get-tuple-element.6) | copy-start | bytes 86020
  73.0 120.3 %reduce-scatter.3.cloned.1.call-start = ((), (), s32[]{:S(2)}) async-start(), calls=%async_computation.2 | async-start | bytes 139264 | tf_op jit(solution)/shard_map/reduce_scatter | solution.py:104
  135.5 59.1 %collective-permute-start.4 = (bf16[16,2048]{1,0:T(8,128)(2,1)S(1)}, bf16[16,2048]{1,0:T(8,128)(2,1)S(1)}, u32[]{:S(2)}, u32[]{:S(2)}) collective-permute-start(bf16[16,2048]{1,0:T(8,128)(2,1)S(1)} %convert_element_type.62), channel_id=1, source_target_pairs={{16,0},{17,1},{18,2},{19,3},{20,4},{21,5},{22,6},{23,7},{24,8},{25... | collective-permute-start | bytes 196616 | tf_op jit(solution)/shard_map/ppermute | solution.py:22
Sparse Core Ops, SparseCore 0:
  12.9 51.3 all-gather.2
  73.1 61.4 reduce-scatter.4
  138.5 54.7 reduce-scatter.2
